TPU v7x, 32 devices: a whole 2x2x4 slice. The times are simulated.
32 devices in a mesh: frame: 8 (over y, x, core), tensor: 4 (over z).
Axes of the slice: x: 2, y: 2, z: 4, core: 2. Of those that a mesh axis runs over, the one named last changes fastest.
Arguments:
- tokens: bfloat16 [1024, 1, 4096], P(('frame', 'tensor')), may hold values from -6 to 6
- norm_gain: float32 [4096], replicated, may hold values from 0.5 to 1.5
- query_weight: bfloat16 [4096, 4096], P(None, 'tensor'), may hold values from -0.09375 to 0.09375
- out_weight: bfloat16 [4096, 4096], P('tensor'), may hold values from -0.09375 to 0.09375
- cache_keys: bfloat16 [384, 1, 4096], P('frame', None, 'tensor'), may hold values from -420 to 420
- cache_values: bfloat16 [384, 1, 4096], P('frame', None, 'tensor'), may hold values from -18 to 18
- token_pos: int32 [1024, 1], P('frame'), may hold values from 0 to 383, as said below
- frame_pad: int32 [1], replicated, may hold values from 0 to 192
Outputs:
- mixed: bfloat16 [1024, 1, 4096], P(('frame', 'tensor'))
Inputs may be any that keep to these rules, and one draw needn't show every extreme that they name: `token_pos`: nondecreasing along each sequence; the last token of every sequence has 383.
All inputs are finite; a program needn't handle non-finite values.
Results may differ from a plain program's by a relative error of at most 0.018.
Values may be sent and summed in bfloat16 or wider, within the bound.
A program may use at most 64 MiB of HBM per device.

v0:
```python
import jax
import jax.numpy as jnp
from jax import lax
from jax.sharding import PartitionSpec as P

HEAD_DIM = 128
epsilon = 1e-06
masked_score = -1e30


def normalize(block_rows, norm_gain):
    hidden = block_rows.astype(jnp.float32)
    factor = lax.rsqrt(jnp.mean(hidden * hidden, axis=-1, keepdims=True) + epsilon)
    return (hidden * factor * norm_gain).astype(jnp.bfloat16)


def per_device(
    tokens, norm_gain, query_weight, out_weight, cache_keys, cache_values, token_pos, frame_pad
):
    head_cols = query_weight.shape[1]
    heads_here = head_cols // HEAD_DIM
    seq_count = tokens.shape[1]
    query_scale = HEAD_DIM ** (-0.5)
    normed = normalize(lax.all_gather(tokens, "tensor", axis=0, tiled=True), norm_gain)
    queries = (
        jnp.dot(normed, query_weight, preferred_element_type=jnp.float32) * query_scale
    ).astype(jnp.bfloat16)
    query_rows = queries.shape[0]
    query_heads = queries.reshape(query_rows, seq_count, heads_here, HEAD_DIM)
    all_frames = cache_keys.shape[0] * lax.axis_size("frame")
    valid_frames = all_frames - frame_pad
    start_max = jnp.full((query_rows, seq_count, heads_here), masked_score, jnp.float32)
    running_max = start_max
    key_piece = lax.all_gather(cache_keys, "frame", axis=0, tiled=True)
    value_piece = lax.all_gather(cache_values, "frame", axis=0, tiled=True)
    row_count = key_piece.shape[0]
    frame_index = jnp.arange(row_count, dtype=jnp.int32)
    visible = (frame_index[None, None, :] <= token_pos[:, :, None]) & (
        frame_index[None, None, :] < valid_frames[None, :, None]
    )
    key_heads = key_piece.reshape(row_count, seq_count, heads_here, HEAD_DIM)
    scores = jnp.einsum(
        "rshd,fshd->rshf", query_heads, key_heads, preferred_element_type=jnp.float32
    )
    visible = visible[:, :, None, :]
    scores, visible = (jnp.where(visible, scores, masked_score), visible)
    new_max = jnp.maximum(running_max, jnp.max(scores, axis=-1))
    weights = jnp.where(visible, jnp.exp(scores - new_max[..., None]), 0.0)
    running_sum = jnp.sum(weights, axis=-1)
    value_heads = value_piece.reshape(value_piece.shape[0], seq_count, heads_here, HEAD_DIM)
    accumulated = jnp.einsum(
        "rshf,fshd->rshd",
        weights.astype(jnp.bfloat16),
        value_heads,
        preferred_element_type=jnp.float32,
    )
    running_max, running_sum, accumulated = (new_max, running_sum, accumulated)
    attended = (
        (accumulated / running_sum[..., None])
        .astype(jnp.bfloat16)
        .reshape(query_rows, seq_count, head_cols)
    )
    return lax.psum_scatter(
        jnp.dot(attended, out_weight, preferred_element_type=jnp.float32).astype(jnp.bfloat16),
        "tensor",
        scatter_dimension=0,
        tiled=True,
    )


def solution(mesh):
    placed = (
        P(("frame", "tensor"), None, None),
        P(),
        P(None, "tensor"),
        P("tensor", None),
        P("frame", None, "tensor"),
        P("frame", None, "tensor"),
        P("frame", None),
        P(),
    )
    return jax.shard_map(
        per_device,
        mesh=mesh,
        in_specs=placed,
        out_specs=P(("frame", "tensor"), None, None),
        check_vma=False,
    )
```

profile of v0, /device:TPU:0, one launch (start us, length us, event | category | flops | bytes accessed | tf_op | source)
XLA Modules:
  0.0 84.1 jit_solution(8908072664769119444)
XLA Ops:
  6.5 0.0 copy-start
  6.5 0.0 all-gather.2.cloned.1.call-start
  6.5 0.7 all-gather.2.cloned.1.call-update
  7.3 0.0 reduce-scatter.2.cloned.1.call-start
  8.0 12.2 %all_gather.10 = bf16[384,1,1024]{2,0,1:T(8,128)(2,1)S(1)} all-gather(bf16[48,1,1024]{2,0,1:T(8,128)(2,1)} %param.12), channel_id=1, replica_groups=mesh['frame'=8,'tensor'=4] {'frame'}, dimensions={0}, use_global_device_ids=true | all-gather | bytes 884736 | tf_op jit(solution)/shard_map/all_gather | solution.py:34
  20.2 0.4 copy.15
  20.5 0.0 copy-done
  20.6 0.0 copy-start.1
  20.6 0.0 copy-start.2
  20.6 10.0 %all_gather.11 = bf16[384,1,1024]{2,0,1:T(8,128)(2,1)S(1)} all-gather(bf16[48,1,1024]{2,0,1:T(8,128)(2,1)S(1)} %copy-done), channel_id=1, replica_groups=mesh['frame'=8,'tensor'=4] {'frame'}, dimensions={0}, use_global_device_ids=true | all-gather | bytes 884736 | tf_op jit(solution)/shard_map/all_gather | solution.py:35
  30.6 0.4 copy.18
  31.0 0.0 copy-done.1
  31.0 0.1 fusion.21
  31.1 8.5 %all-gather.2.cloned.1.call-done = bf16[128,1,4096]{2,0,1:T(8,128)(2,1)} async-done(((bf16[32,1,4096]{2,0,1:T(8,128)(2,1)}), bf16[128,1,4096]{2,0,1:T(8,128)(2,1)}) %all-gather.2.cloned.1.call-update) | async-done | bytes 1048592 | tf_op jit(solution)/shard_map/all_gather | solution.py:24
  39.6 0.0 slice-start
  39.6 1.7 %fusion.1 = f32[128]{0:T(128)S(1)} fusion(bf16[128,1,4096]{2,0,1:T(8,128)(2,1)} %all-gather.2.cloned.1.call-done), kind=kLoop, calls=%fused_computation.4 | loop fusion | flops 1572736 | bytes 1049088 | tf_op jit(solution)/shard_map/reduce_sum | solution.py:13
  41.3 0.0 copy-done.2
  41.3 0.0 slice-start.1
  41.3 5.2 %fusion.7 = bf16[16,8,8,128]{3,2,1,0:T(8,128)(2,1)S(1)} fusion(bf16[4096,1024]{1,0:T(8,128)(2,1)} %param.10, bf16[128,1,4096]{2,0,1:T(8,128)(2,1)} %all-gather.2.cloned.1.call-done, f32[4096]{0:T(1024)S(1)} %copy-done.2, f32[128]{0:T(128)S(1)} %add_rsqrt_fusion), kind=kOutput, calls=%fused_computation.14 | convolution fusion | flops 1076101120 | bytes 9716224 | tf_op jit(solution)/shard_map/dot_general | solution.py:26
  46.5 0.5 fusion.23
  47.0 0.6 fusion.4
  47.6 0.6 fusion.13
  48.1 0.0 slice-done
  48.2 0.0 slice-done.1
  48.2 2.3 %fusion = bf16[128,1,4096]{2,0,1:T(8,128)(2,1)} fusion(bf16[128,1024]{0,1:T(8,128)(2,1)S(1)} %bitcast.45, bf16[1024,4096]{1,0:T(8,128)(2,1)S(1)} %bitcast.42), kind=kOutput, calls=%fused_computation.1 | convolution fusion | flops 1074266112 | bytes 9699328 | tf_op jit(solution)/shard_map/dot_general | solution.py:64
  50.4 0.0 reduce-scatter.2.cloned.1.call-update
  50.5 26.8 %reduce-scatter.2.cloned.1.call-done = bf16[32,1,4096]{2,0,1:T(8,128)(2,1)} async-done(((bf16[128,1,4096]{2,0,1:T(8,128)(2,1)}), bf16[32,1,4096]{2,0,1:T(8,128)(2,1)}) %reduce-scatter.2.cloned.1.call-update) | async-done | bytes 262160 | tf_op jit(solution)/shard_map/reduce_scatter | solution.py:63
  (4 shorter events, 0.0 us)
Async XLA Ops:
  6.5 14.0 %copy-start = (bf16[48,1,1024]{2,0,1:T(8,128)(2,1)S(1)}, bf16[48,1,1024]{2,0,1:T(8,128)(2,1)}, u32[]{:S(2)}) copy-start(bf16[48,1,1024]{2,0,1:T(8,128)(2,1)} %param.13) | copy-start | bytes 294916
  6.5 33.1 %all-gather.2.cloned.1.call-start = ((), (), s32[]{:S(2)}) async-start(), calls=%async_computation.1 | async-start | bytes 1310720 | tf_op jit(solution)/shard_map/all_gather | solution.py:24
  7.3 70.0 %reduce-scatter.2.cloned.1.call-start = ((), (), s32[]{:S(2)}) async-start(), calls=%async_computation.2 | async-start | bytes 1310720 | tf_op jit(solution)/shard_map/reduce_scatter | solution.py:63
  20.6 10.4 %copy-start.1 = (s32[128,1]{0,1:T(1,128)S(1)}, s32[128,1]{0,1:T(1,128)}, u32[]{:S(2)}) copy-start(s32[128,1]{0,1:T(1,128)} %param.14) | copy-start | bytes 1540
  20.6 20.8 %copy-start.2 = (f32[4096]{0:T(1024)S(1)}, f32[4096]{0:T(1024)}, u32[]{:S(2)}) copy-start(f32[4096]{0:T(1024)} %param.9) | copy-start | bytes 49156
  39.6 8.5 %slice-start = ((s8[8388608]{0:T(1024)(128)(4,1)}), s8[4194304]{0:T(1024)(128)(4,1)S(1)}, s32[]{:S(2)}) async-start(s8[8388608]{0:T(1024)(128)(4,1)} %bitcast.41), calls=%async_computation.3 | async-start | bytes 8388608
  41.3 6.8 %slice-start.1 = ((s8[8388608]{0:T(1024)(128)(4,1)}), s8[4194304]{0:T(1024)(128)(4,1)S(1)}, s32[]{:S(2)}) async-start(s8[8388608]{0:T(1024)(128)(4,1)} %bitcast.41), calls=%async_computation.4 | async-start | bytes 8388608
Sparse Core Ops, SparseCore 0:
  8.9 30.6 all-gather.1
  50.6 26.6 reduce-scatter.1
where the time goes:
time: 84.3 us; the launch traced here: 84.1 us
  waiting for transfers between devices  36.1 us (43%)
  blocking collectives  22.3 us (26%)
  between operations  14.2 us (17%)
  matrix products  8.47 us (10%)
  other arithmetic  2.36 us (3%)
    reduce_scatter x1, waiting for transfers between devices, per_device(): lax.psum_scatter(jnp.dot(attended, out_weight, preferred_element_type=jnp...  26.8 us
    all_gather x1, blocking collectives, per_device(): key_piece = lax.all_gather(cache_keys, 'frame', axis=0, tiled=True)  12.2 us
    all_gather x1, blocking collectives, per_device(): value_piece = lax.all_gather(cache_values, 'frame', axis=0, tiled=True)  10 us
    all_gather x1, waiting for transfers between devices, per_device(): lax.all_gather(tokens, 'tensor', axis=0, tiled=True)  8.55 us
    dot_general x1, matrix products, per_device(): jnp.dot(normed, query_weight, preferred_element_type=jnp.float32)  5.17 us
    dot_general x1, matrix products, per_device(): jnp.dot(attended, out_weight, preferred_element_type=jnp.float32)  2.26 us
  transfers between devices with their start and end apart: 2, of which 2 were waited for; matrix products, arithmetic and copies ran while one was open for 1% of the time, Pallas kernels for 0%

commit v1 on v0

--- a/solution.py
+++ b/solution.py
@@ -17,6 +17,15 @@
 def per_device(
     tokens, norm_gain, query_weight, out_weight, cache_keys, cache_values, token_pos, frame_pad
 ):
+
+    def _store_arrays(a0, shard_in):
+        carry_in = jnp.split(
+            lax.all_gather(jnp.concatenate([a0, shard_in], axis=1), "frame", axis=0, tiled=True),
+            [a0.shape[1]],
+            axis=1,
+        )
+        return carry_in
+
     head_cols = query_weight.shape[1]
     heads_here = head_cols // HEAD_DIM
     seq_count = tokens.shape[1]
@@ -31,8 +40,7 @@
     valid_frames = all_frames - frame_pad
     start_max = jnp.full((query_rows, seq_count, heads_here), masked_score, jnp.float32)
     running_max = start_max
-    key_piece = lax.all_gather(cache_keys, "frame", axis=0, tiled=True)
-    value_piece = lax.all_gather(cache_values, "frame", axis=0, tiled=True)
+    key_piece, value_piece = _store_arrays(cache_keys, cache_values)
     row_count = key_piece.shape[0]
     frame_index = jnp.arange(row_count, dtype=jnp.int32)
     visible = (frame_index[None, None, :] <= token_pos[:, :, None]) & (

time: 84.3 us -> 117 us (1.39)
  waiting for transfers between devices: 36.1 us -> 77.4 us
  blocking collectives: 22.3 us -> 0 us
  local copies, waits for them, and re-layouts: 0.73 us -> 9.78 us
  matrix products: 8.47 us -> 11.5 us
  other arithmetic: 2.36 us -> 3.55 us
    all_gather x2 -> x0, blocking collectives: 22.3 us -> none  [the longest x1 12.2 us: per_device(): key_piece = lax.all_gather(cache_keys, 'frame', axis=0, tiled=True)]
    all_gather x1, waiting for transfers between devices: 8.55 us -> 29 us  [per_device(): lax.all_gather(tokens, 'tensor', axis=0, tiled=True)]
    all_gather x0 -> x1, waiting for transfers between devices: none -> 20.3 us  [_store_arrays(): lax.all_gather(jnp.concatenate([a0, shard_in], axis=1), 'frame', axis=0,...]
    split x0 -> x2, local copies, waits for them, and re-layouts: none -> 7.22 us  [_store_arrays(): jnp.split(lax.all_gather(jnp.concatenate([a0, shard_in], axis=1), 'frame'...]
    dot_general x1, matrix products: 2.26 us -> 5.66 us  [per_device(): jnp.dot(attended, out_weight, preferred_element_type=jnp.float32)]
    unnamed x10 -> x5, local copies, waits for them, and re-layouts: 0.03 us -> 1.68 us
  transfers between devices with their start and end apart: 2 -> 3, of which waited for: 2 -> 3; matrix products, arithmetic and copies ran while one was open for 1% -> 8% of each run, Pallas kernels for 0% -> 0%
where the time goes in v1:
time: 117 us; the launch traced here: 116 us
  waiting for transfers between devices  77.4 us (66%)
  between operations  13.8 us (12%)
  matrix products  11.5 us (10%)
  local copies, waits for them, and re-layouts  9.78 us (8%)
  other arithmetic  3.55 us (3%)
    all_gather x1, waiting for transfers between devices, per_device(): lax.all_gather(tokens, 'tensor', axis=0, tiled=True)  29 us
    reduce_scatter x1, waiting for transfers between devices, per_device(): lax.psum_scatter(jnp.dot(attended, out_weight, preferred_element_type=jnp...  27.4 us
    all_gather x1, waiting for transfers between devices, _store_arrays(): lax.all_gather(jnp.concatenate([a0, shard_in], axis=1), 'frame', axis=0,...  20.3 us
    split x2, local copies, waits for them, and re-layouts, _store_arrays(): jnp.split(lax.all_gather(jnp.concatenate([a0, shard_in], axis=1), 'frame'...  7.22 us
    dot_general x1, matrix products, per_device(): jnp.dot(attended, out_weight, preferred_element_type=jnp.float32)  5.66 us
    dot_general x1, matrix products, per_device(): jnp.dot(normed, query_weight, preferred_element_type=jnp.float32)  5.04 us
  transfers between devices with their start and end apart: 3, of which 3 were waited for; matrix products, arithmetic and copies ran while one was open for 8% of the time, Pallas kernels for 0%

profile of v1, /device:TPU:0, one launch (start us, length us, event | category | flops | bytes accessed | tf_op | source)
XLA Modules:
  0.0 116.2 jit_solution(6860940489041761363)
XLA Ops:
  6.5 0.0 copy-start.1
  6.5 0.0 all-gather.5.cloned.1.call-start
  6.5 0.7 all-gather.5.cloned.1.call-update
  7.3 0.0 all-gather.3.cloned.1.call-start
  7.3 1.0 pad_maximum_fusion
  8.3 0.9 copy.17
  9.1 0.0 all-gather.3.cloned.1.call-update
  9.2 0.0 reduce-scatter.2.cloned.1.call-start
  9.9 0.8 fusion.21
  10.7 29.0 %all-gather.5.cloned.1.call-done = bf16[128,1,4096]{2,0,1:T(8,128)(2,1)} async-done(((bf16[32,1,4096]{2,0,1:T(8,128)(2,1)}), bf16[128,1,4096]{2,0,1:T(8,128)(2,1)}) %all-gather.5.cloned.1.call-update) | async-done | bytes 1048592 | tf_op jit(solution)/shard_map/all_gather | solution.py:33
  39.6 1.5 %fusion.1 = f32[128]{0:T(128)S(1)} fusion(bf16[128,1,4096]{2,0,1:T(8,128)(2,1)} %all-gather.5.cloned.1.call-done), kind=kLoop, calls=%fused_computation.4 | loop fusion | flops 1572736 | bytes 1049088 | tf_op jit(solution)/shard_map/reduce_sum | solution.py:13
  41.2 0.0 copy-done.1
  41.2 5.0 %fusion.7 = bf16[16,8,8,128]{3,2,1,0:T(8,128)(2,1)S(1)} fusion(bf16[4096,1024]{1,0:T(8,128)(2,1)} %param.10, bf16[128,1,4096]{2,0,1:T(8,128)(2,1)} %all-gather.5.cloned.1.call-done, f32[4096]{0:T(1024)S(1)} %copy-done.1, f32[128]{0:T(128)S(1)} %add_rsqrt_fusion), kind=kOutput, calls=%fused_computation.14 | convolution fusion | flops 1076101120 | bytes 9716224 | tf_op jit(solution)/shard_map/dot_general | solution.py:35
  46.2 20.3 %all-gather.3.cloned.1.call-done = bf16[384,2,1024]{2,1,0:T(2,128)(2,1)} async-done(((bf16[48,2,1024]{2,1,0:T(2,128)(2,1)}), bf16[384,2,1024]{2,1,0:T(2,128)(2,1)}) %all-gather.3.cloned.1.call-update) | async-done | bytes 1572880 | tf_op jit(solution)/shard_map/all_gather | solution.py:23
  66.5 4.4 %fusion.23 = (bf16[384,1,1024]{2,1,0:T(2,128)(2,1)S(1)}, bf16[384,1,1024]{2,1,0:T(2,128)(2,1)S(1)}) fusion(bf16[384,2,1024]{2,1,0:T(2,128)(2,1)} %all-gather.3.cloned.1.call-done), kind=kLoop, calls=%fused_computation.33 | loop fusion | bytes 3145728 | tf_op jit(solution)/shard_map/split | solution.py:22
  70.9 2.8 %copy.18 = bf16[384,1,1024]{0,2,1:T(8,128)(2,1)} copy(bf16[384,1,1024]{2,1,0:T(2,128)(2,1)S(1)} %get-tuple-element.6) | data formatting | bytes 1572864 | tf_op jit(solution)/shard_map/split | solution.py:22
  73.7 1.3 %copy.25 = bf16[384,1,1024]{0,2,1:T(8,128)(2,1)S(1)} copy(bf16[384,1,1024]{2,1,0:T(2,128)(2,1)S(1)} %get-tuple-element.5) | data formatting | bytes 1572864
  75.0 0.0 copy-start
  75.0 0.4 fusion.24
  75.5 0.3 fusion.4
  75.8 0.4 copy-done
  76.2 0.4 fusion.13
  76.6 5.7 %fusion = bf16[128,1,4096]{2,0,1:T(8,128)(2,1)} fusion(bf16[128,1024]{0,1:T(8,128)(2,1)S(1)} %bitcast.39, bf16[1024,4096]{1,0:T(8,128)(2,1)} %param.11), kind=kOutput, calls=%fused_computation.1 | convolution fusion | flops 1074266112 | bytes 9699328 | tf_op jit(solution)/shard_map/dot_general | solution.py:72
  82.2 0.0 reduce-scatter.2.cloned.1.call-update
  82.3 27.4 %reduce-scatter.2.cloned.1.call-done = bf16[32,1,4096]{2,0,1:T(8,128)(2,1)} async-done(((bf16[128,1,4096]{2,0,1:T(8,128)(2,1)}), bf16[32,1,4096]{2,0,1:T(8,128)(2,1)}) %reduce-scatter.2.cloned.1.call-update) | async-done | bytes 262160 | tf_op jit(solution)/shard_map/reduce_scatter | solution.py:71
  (3 shorter events, 0.0 us)
Async XLA Ops:
  6.5 34.6 %copy-start.1 = (f32[4096]{0:T(1024)S(1)}, f32[4096]{0:T(1024)}, u32[]{:S(2)}) copy-start(f32[4096]{0:T(1024)} %param.9) | copy-start | bytes 49156
  6.5 33.1 %all-gather.5.cloned.1.call-start = ((), (), s32[]{:S(2)}) async-start(), calls=%async_computation.2 | async-start | bytes 1310720 | tf_op jit(solution)/shard_map/all_gather | solution.py:33
  7.3 59.2 %all-gather.3.cloned.1.call-start = ((), (), s32[]{:S(2)}) async-start(), calls=%async_computation.1 | async-start | bytes 1769472 | tf_op jit(solution)/shard_map/all_gather | solution.py:23
  9.2 100.5 %reduce-scatter.2.cloned.1.call-start = ((), (), s32[]{:S(2)}) async-start(), calls=%async_computation.3 | async-start | bytes 1310720 | tf_op jit(solution)/shard_map/reduce_scatter | solution.py:71
  75.0 1.1 copy-start
Sparse Core Ops, SparseCore 0:
  8.9 30.6 all-gather.4
  41.5 24.9 all-gather.2
  82.4 27.2 reduce-scatter.1
